TPU v7x, 256 devices: a whole 4x4x8 slice. The times are simulated.
256 devices in a mesh: row: 16 (over x_hi, z), col: 16 (over y, x_lo, core).
Axes of the slice: x: 4 (x_hi: 2, x_lo: 2; x = x_hi * 2 + x_lo), y: 4, z: 8, core: 2. Of those that a mesh axis runs over, the one named last changes fastest.
Arguments:
- signal: float32 [8192, 16384], P('row', 'col'), may hold values from -6 to 6
- apod: float32 [8192], P('row'), may hold values from 0.3 to 1
- coef: float32 [4, 16384], P(None, 'col'), may hold values from -0.5 to 1
- block_offset: int32 [512], P('col'), may hold values from -16 to 9
- fine_start: int32 [16384], P('col'), may hold values from 0 to 3
Outputs:
- calibrated: float32 [2, 8192, 16384], P(None, 'row', 'col')
All inputs are finite; a program needn't handle non-finite values.
Results may differ from a plain program's by a relative error of at most 0.000084.
Values sent between devices are 32-bit elements; how exact they have to be, the bound alone decides.
A program may use at most 128 MiB of HBM per device.

v0:
```python
import math

import jax
import jax.numpy as jnp
from jax import lax
from jax.sharding import PartitionSpec as P

TAPS = 4
HALO = 16


HIGH = lax.Precision.HIGHEST


def padded_2(value, sides, width):
    for axis, dim in sides:
        count, length = (lax.axis_size(axis), value.shape[dim])
        up = [(i, (i + 1) % count) for i in range(count - 1)]
        down = [(j, i) for i, j in up]
        last = lax.slice_in_dim(value, length - width, length, axis=dim)
        first = lax.slice_in_dim(value, 0, width, axis=dim)
        before = lax.ppermute(last, axis, up)
        after = lax.ppermute(first, axis, down)
        value = jnp.concatenate([before, value, after], axis=dim)
    return value


def cut_along(value, dim, count):
    dims = value.shape
    parts = value.reshape(*dims[:dim], count, dims[dim] // count, *dims[dim + 1 :])
    return jnp.moveaxis(parts, dim, 0)


def piece_ends(length, count):
    step = length // count
    if step >= 8:
        step -= step % 8
    return [step * k for k in range(1, count)]


def laid_out(parts, dim):
    parts = jnp.moveaxis(parts, 0, dim)
    dims = parts.shape
    return parts.reshape(*dims[:dim], dims[dim] * dims[dim + 1], *dims[dim + 2 :])


def several_exchanges(value, axis, pieces, split_dim, concat_dim):
    parts = cut_along(value, split_dim, lax.axis_size(axis))
    split_at = max(range(1, max(2, parts.ndim - 1)), key=lambda d: parts.shape[d])
    done = []
    for share in jnp.split(parts, piece_ends(parts.shape[split_at], pieces), axis=split_at):
        if share.size:
            done.append(lax.all_to_all(share, axis, split_axis=0, concat_axis=0, tiled=True))
    return laid_out(jnp.concatenate(done, axis=split_at), concat_dim)


def digits_reversed(values, levels):
    result = jnp.zeros_like(values)
    for digit in range(levels):
        result = result + ((values >> digit & 1) << levels - 1 - digit)
    return result


def band_starts(block_offset, fine_start, width):
    blocks = block_offset.shape[0]
    spread = jnp.broadcast_to(block_offset[:, None], (blocks, width // blocks)).reshape(width)
    return jnp.arange(width, dtype=jnp.int32) + spread + fine_start + HALO


def apply_stencil(padded, coef, first):
    width = first.shape[0]
    total = jnp.zeros(padded.shape[:-1] + (width,), jnp.float32)
    for tap in range(TAPS):
        total = total + coef[tap] * jnp.take(padded, first + tap, axis=-1)
    return total


def inner_tables(count, total):
    index = jnp.arange(count, dtype=jnp.int32)
    angle = 2.0 * math.pi / count * (index[:, None] * index[None, :] % count).astype(jnp.float32)
    scale = 1.0 / math.sqrt(total)
    return (jnp.cos(angle) * scale, jnp.sin(angle) * scale)


def on_device(signal, apod, coef, block_offset, fine_start):
    local_rows, width = signal.shape
    devices = lax.axis_size("row")
    levels = devices.bit_length() - 1
    total = local_rows * devices
    first = band_starts(block_offset, fine_start, width)
    field = signal * apod[:, None]
    padded = padded_2(field, (("col", 1),), HALO)
    field = apply_stencil(padded, coef, first)
    cosine, sine = inner_tables(local_rows, total)
    positions = jnp.arange(local_rows, dtype=jnp.int32)
    gathered = lax.all_to_all(field, "row", split_axis=1, concat_axis=0, tiled=True)
    blocks = gathered.reshape(devices, local_rows, gathered.shape[1])
    outer = digits_reversed(jnp.arange(devices, dtype=jnp.int32), levels)
    outer_angle = (
        2.0
        * math.pi
        / devices
        * (outer[:, None] * jnp.arange(devices, dtype=jnp.int32)[None, :] % devices).astype(
            jnp.float32
        )
    )
    real_part = jnp.einsum(
        "ir,rmc->imc",
        jnp.cos(outer_angle),
        blocks,
        precision=HIGH,
        preferred_element_type=jnp.float32,
    )
    imag_part = -jnp.einsum(
        "ir,rmc->imc",
        jnp.sin(outer_angle),
        blocks,
        precision=HIGH,
        preferred_element_type=jnp.float32,
    )
    angle = (
        2.0 * math.pi / total * (outer[:, None] * positions[None, :] % total).astype(jnp.float32)
    )
    turn_cos = jnp.cos(angle)[:, :, None]
    turn_sin = jnp.sin(angle)[:, :, None]
    rotated_re = real_part * turn_cos + imag_part * turn_sin
    rotated_im = imag_part * turn_cos - real_part * turn_sin
    real_out = jnp.einsum(
        "km,imc->ikc", cosine, rotated_re, precision=HIGH, preferred_element_type=jnp.float32
    ) + jnp.einsum(
        "km,imc->ikc", sine, rotated_im, precision=HIGH, preferred_element_type=jnp.float32
    )
    imag_out = jnp.einsum(
        "km,imc->ikc", cosine, rotated_im, precision=HIGH, preferred_element_type=jnp.float32
    ) - jnp.einsum(
        "km,imc->ikc", sine, rotated_re, precision=HIGH, preferred_element_type=jnp.float32
    )
    stacked = jnp.stack([real_out.reshape(total, -1), imag_out.reshape(total, -1)])
    result = several_exchanges(stacked, "row", 2, 1, 2)
    return result


def solution(mesh):
    placed = (P("row", "col"), P("row"), P(None, "col"), P("col"), P("col"))
    return jax.shard_map(
        on_device, mesh=mesh, in_specs=placed, out_specs=P(None, "row", "col"), check_vma=False
    )
```

profile of v0, /device:TPU:8, one launch (start us, length us, event | category | flops | bytes accessed | tf_op | source)
XLA Modules:
  0.0 268.0 jit_solution(10340520118512865120)
XLA Ops:
  0.0 1.9 copy.27
  3.6 1.9 collective-permute-start
  5.5 4.5 %collective-permute-start.1 = (f32[512,16]{0,1:T(8,128)S(1)}, f32[512,16]{0,1:T(8,128)S(1)}, u32[]{:S(2)}, u32[]{:S(2)}) collective-permute-start(f32[512,16]{0,1:T(8,128)S(1)} %get-tuple-element.13), channel_id=1, source_target_pairs={{1,0},{2,1},{3,2},{4,3},{5,4},{6,5},{7,6},{8,7},{9,8},{10,9},{11,1... | collective-permute-start | bytes 98312 | tf_op jit(solution)/shard_map/ppermute | solution.py:23
  11.6 1.8 pad_maximum_fusion.1
  13.4 4.9 %gather_fusion = f32[1024,512]{1,0:T(8,128)} fusion(f32[512,1056]{0,1:T(8,128)S(1)} %pad_maximum_fusion.1, s32[1024]{0:T(1024)S(1)} %get-tuple-element.21), kind=kCustom, calls=%fused_computation.clone | custom fusion | bytes 4198400 | tf_op jit(solution)/shard_map/jit(_take)/gather | solution.py:74
  18.3 4.9 %gather_fusion.1 = f32[1024,512]{1,0:T(8,128)} fusion(f32[512,1056]{0,1:T(8,128)S(1)} %pad_maximum_fusion.1, s32[1024]{0:T(1024)S(1)} %get-tuple-element.24), kind=kCustom, calls=%fused_computation.1.clone | custom fusion | bytes 4198400 | tf_op jit(solution)/shard_map/jit(_take)/gather | solution.py:74
  23.2 4.9 %gather_fusion.2 = f32[1024,512]{1,0:T(8,128)} fusion(f32[512,1056]{0,1:T(8,128)S(1)} %pad_maximum_fusion.1, s32[1024]{0:T(1024)S(1)} %get-tuple-element.23), kind=kCustom, calls=%fused_computation.2.clone | custom fusion | bytes 4198400 | tf_op jit(solution)/shard_map/jit(_take)/gather | solution.py:74
  28.1 4.9 %gather_fusion.3 = f32[1024,512]{1,0:T(8,128)} fusion(f32[512,1056]{0,1:T(8,128)S(1)} %pad_maximum_fusion.1, s32[1024]{0:T(1024)S(1)} %get-tuple-element.22), kind=kCustom, calls=%fused_computation.3.clone | custom fusion | bytes 4198400 | tf_op jit(solution)/shard_map/jit(_take)/gather | solution.py:74
  33.0 5.8 %fusion.4 = f32[512,1024]{0,1:T(8,128)} fusion(f32[1024,512]{1,0:T(8,128)} %gather_fusion.3, f32[1024,512]{1,0:T(8,128)} %gather_fusion.2, f32[1024,512]{1,0:T(8,128)} %gather_fusion.1, f32[1024,512]{1,0:T(8,128)} %gather_fusion, f32[1024]{0:T(1024)S(1)} %bitcast.67, f32[1024]{0:T(1024)S(1)} %bitcast.68, f32[1024]{0:T(1024)S(1)} %bitcast.66, ...), kind=kLoop, calls=%fused_computation.12 | loop fusion | flops 5767168 | bytes 10506240 | tf_op jit(solution)/shard_map/add | solution.py:74
  38.7 11.2 %all-to-all-start = ((f32[512,16,64]{0,2,1:T(8,128)}), f32[512,16,64]{0,2,1:T(8,128)S(1)}, u32[]{:S(2)}, u32[]{:S(2)}) async-start(f32[512,16,64]{0,2,1:T(8,128)} %bitcast.64), calls=%async_computation | async-start | bytes 4194304 | tf_op jit(solution)/shard_map/all_to_all | solution.py:96
  50.2 50.2 %all-to-all-done = f32[512,16,64]{0,2,1:T(8,128)S(1)} async-done(((f32[512,16,64]{0,2,1:T(8,128)}), f32[512,16,64]{0,2,1:T(8,128)S(1)}, u32[]{:S(2)}, u32[]{:S(2)}) %all-to-all-start) | async-done | bytes 2097184 | tf_op jit(solution)/shard_map/all_to_all | solution.py:96
  100.4 2.9 %fusion = f32[16,512,64]{1,0,2:T(8,128)S(1)} fusion(f32[512,16,64]{0,2,1:T(8,128)S(1)} %all-to-all-done, s32[16]{0:T(128)S(1)} %fusion.67), kind=kOutput, calls=%fused_computation.7 | convolution fusion | flops 100666880 | bytes 4194368 | tf_op jit(solution)/shard_map/ir,rmc->imc/dot_general | solution.py:114
  103.3 3.4 %multiply_add_fusion = (f32[16,512,64]{1,0,2:T(8,128)S(1)}, f32[16,512,64]{1,0,2:T(8,128)S(1)}) fusion(f32[16,512,64]{1,0,2:T(8,128)S(1)} %fusion, f32[16,512]{1,0:T(8,128)S(1)} %get-tuple-element.26, f32[16,512]{1,0:T(8,128)S(1)} %get-tuple-element.25, f32[512,16,64]{0,2,1:T(8,128)S(1)} %all-to-all-done, s32[16]{0:T(128)S(1)} %fusion.67), kind=kOutput, calls=%fused_computation.21 | convolution fusion | flops 104336896 | bytes 8454208 | tf_op jit(solution)/shard_map/ir,rmc->imc/dot_general | solution.py:107
  106.7 8.4 %fusion.9 = f32[16,64,512]{2,1,0:T(8,128)S(1)} fusion(f32[16,512,64]{1,0,2:T(8,128)S(1)} %get-tuple-element.9), kind=kOutput, calls=%fused_computation.24 | convolution fusion | flops 3225157632 | bytes 4194304 | tf_op jit(solution)/shard_map/km,imc->ikc/dot_general | solution.py:130
  115.1 8.2 %fusion.7 = f32[16,64,512]{2,1,0:T(8,128)S(1)} fusion(f32[16,512,64]{1,0,2:T(8,128)S(1)} %get-tuple-element.9), kind=kOutput, calls=%fused_computation.22 | convolution fusion | flops 3225157632 | bytes 4194304 | tf_op jit(solution)/shard_map/km,imc->ikc/dot_general | solution.py:133
  123.3 8.6 %add_bitcast_fusion = f32[1,16,512,64]{2,3,1,0:T(8,128)S(1)} fusion(f32[16,64,512]{2,1,0:T(8,128)S(1)} %fusion.9, f32[16,512,64]{1,0,2:T(8,128)S(1)} %get-tuple-element.8), kind=kOutput, calls=%fused_computation.19 | convolution fusion | flops 3225681920 | bytes 6291456 | tf_op jit(solution)/shard_map/km,imc->ikc/dot_general | solution.py:128
  131.9 8.4 %subtract_bitcast_fusion = f32[1,16,512,64]{2,3,1,0:T(8,128)S(1)} fusion(f32[16,64,512]{2,1,0:T(8,128)S(1)} %fusion.7, f32[16,512,64]{1,0,2:T(8,128)S(1)} %get-tuple-element.8), kind=kOutput, calls=%fused_computation.18 | convolution fusion | flops 3225681920 | bytes 6291456 | tf_op jit(solution)/shard_map/km,imc->ikc/dot_general | solution.py:135
  141.0 1.8 fusion.102
  144.4 7.0 %all-to-all-start.1 = ((f32[16,2,256,64]{2,3,1,0:T(8,128)}), f32[16,2,256,64]{2,3,1,0:T(8,128)}, u32[]{:S(2)}, u32[]{:S(2)}) async-start(f32[16,2,256,64]{2,3,1,0:T(8,128)} %copy.33), calls=%async_computation.1 | async-start | bytes 4194304 | tf_op jit(solution)/shard_map/all_to_all | solution.py:53
  153.1 48.7 %all-to-all-done.1 = f32[16,2,256,64]{2,3,1,0:T(8,128)} async-done(((f32[16,2,256,64]{2,3,1,0:T(8,128)}), f32[16,2,256,64]{2,3,1,0:T(8,128)}, u32[]{:S(2)}, u32[]{:S(2)}) %all-to-all-start.1) | async-done | bytes 2097184 | tf_op jit(solution)/shard_map/all_to_all | solution.py:53
  201.8 56.0 %all_to_all.26 = f32[16,2,256,64]{2,3,1,0:T(8,128)S(1)} all-to-all(f32[16,2,256,64]{2,3,1,0:T(8,128)S(1)} %copy.34), channel_id=1, replica_groups=mesh['row'=16,'col'=16] {'row'}, dimensions={0} | all-to-all | bytes 4194304 | tf_op jit(solution)/shard_map/all_to_all | solution.py:53
  257.8 2.1 pad_maximum_fusion
  260.0 2.5 copy.38
  262.5 5.3 %copy.37 = f32[2,512,1024]{2,1,0:T(8,128)} copy(f32[2,512,1024]{1,2,0:T(8,128)} %bitcast.63) | data formatting | bytes 8388608 | tf_op jit(solution)/shard_map/reshape | solution.py:44
  (25 shorter events, 7.3 us)
Async XLA Ops:
  0.0 1.9 copy-start.3
  2.0 8.1 %copy-start.4 = (s32[32]{0:T(128)S(1)}, s32[32]{0:T(128)}, u32[]{:S(2)}) copy-start(s32[32]{0:T(128)} %param.10) | copy-start | bytes 388
  2.0 8.2 %copy-start.2 = (s32[1024]{0:T(1024)S(1)}, s32[1024]{0:T(1024)}, u32[]{:S(2)}) copy-start(s32[1024]{0:T(1024)} %param.11) | copy-start | bytes 12292
  2.0 8.2 %copy-start.1 = (f32[4,1024]{1,0:T(4,128)S(1)}, f32[4,1024]{1,0:T(4,128)}, u32[]{:S(2)}) copy-start(f32[4,1024]{1,0:T(4,128)} %param.9) | copy-start | bytes 49156
  2.2 1.3 copy-start
  3.6 6.7 %collective-permute-start = (f32[512,16]{0,1:T(8,128)S(1)}, f32[512,16]{0,1:T(8,128)S(1)}, u32[]{:S(2)}, u32[]{:S(2)}) collective-permute-start(f32[512,16]{0,1:T(8,128)S(1)} %get-tuple-element.12), channel_id=1, source_target_pairs={{0,1},{1,2},{2,3},{3,4},{4,5},{5,6},{6,7},{7,8},{8,9},{9,10},{10,1... | collective-permute-start | bytes 98312 | tf_op jit(solution)/shard_map/ppermute | solution.py:22
  5.5 6.1 %collective-permute-start.1 = (f32[512,16]{0,1:T(8,128)S(1)}, f32[512,16]{0,1:T(8,128)S(1)}, u32[]{:S(2)}, u32[]{:S(2)}) collective-permute-start(f32[512,16]{0,1:T(8,128)S(1)} %get-tuple-element.13), channel_id=1, source_target_pairs={{1,0},{2,1},{3,2},{4,3},{5,4},{6,5},{7,6},{8,7},{9,8},{10,9},{11,1... | collective-permute-start | bytes 98312 | tf_op jit(solution)/shard_map/ppermute | solution.py:23
  38.7 61.7 %all-to-all-start = ((f32[512,16,64]{0,2,1:T(8,128)}), f32[512,16,64]{0,2,1:T(8,128)S(1)}, u32[]{:S(2)}, u32[]{:S(2)}) async-start(f32[512,16,64]{0,2,1:T(8,128)} %bitcast.64), calls=%async_computation | async-start | bytes 4194304 | tf_op jit(solution)/shard_map/all_to_all | solution.py:96
  144.4 57.4 %all-to-all-start.1 = ((f32[16,2,256,64]{2,3,1,0:T(8,128)}), f32[16,2,256,64]{2,3,1,0:T(8,128)}, u32[]{:S(2)}, u32[]{:S(2)}) async-start(f32[16,2,256,64]{2,3,1,0:T(8,128)} %copy.33), calls=%async_computation.1 | async-start | bytes 4194304 | tf_op jit(solution)/shard_map/all_to_all | solution.py:53
where the time goes:
time: 271 us; the launch traced here: 268 us
  waiting for transfers between devices  100 us (37%)
  blocking collectives  56 us (21%)
  matrix products  39.9 us (15%)
  local copies, waits for them, and re-layouts  35.9 us (13%)
  starting transfers between devices  24.6 us (9%)
  other arithmetic  10.9 us (4%)
    all_to_all x1, blocking collectives, several_exchanges(): lax.all_to_all(share, axis, split_axis=0, concat_axis=0, tiled=True)  56 us
    all_to_all x1, waiting for transfers between devices, on_device(): lax.all_to_all(field, 'row', split_axis=1, concat_axis=0, tiled=True)  50.2 us
    all_to_all x1, waiting for transfers between devices, several_exchanges(): lax.all_to_all(share, axis, split_axis=0, concat_axis=0, tiled=True)  48.7 us
    gather x4, local copies, waits for them, and re-layouts, apply_stencil(): total = total + coef[tap] * jnp.take(padded, first + tap, axis=-1)  19.6 us
    all_to_all x1, starting transfers between devices, on_device(): lax.all_to_all(field, 'row', split_axis=1, concat_axis=0, tiled=True)  11.2 us
    dot_general x1, matrix products, on_device(): jnp.einsum('km,imc->ikc', cosine, rotated_re, precision=HIGH, preferred_e...  8.6 us
    dot_general x1, matrix products, on_device(): jnp.einsum('km,imc->ikc', sine, rotated_im, precision=HIGH, preferred_ele...  8.4 us
    dot_general x1, matrix products, on_device(): jnp.einsum('km,imc->ikc', sine, rotated_re, precision=HIGH, preferred_ele...  8.39 us
  transfers between devices with their start and end apart: 4, of which 3 were waited for; matrix products, arithmetic and copies ran while one was open for 1% of the time, Pallas kernels for 0%

commit v1 on v0

v1 whole, which is shorter than its diff:
```python
import functools
import math

import jax
import jax.numpy as jnp
from jax import lax
from jax.experimental import pallas as pl
from jax.experimental.pallas import tpu as pltpu
from jax.sharding import PartitionSpec as P

MESH = pl.DeviceIdType.MESH
TAPS = 4
NZ = 8
NB = 8
LANES = 128
ROWS = 512
SLAB = ROWS // NZ
WIDE = NB * LANES
T1 = 8192
F32, BF16 = jnp.float32, jnp.bfloat16

BASE = ((0, 4, 6, 2), (1, 9, 5, 13))
PAIR_OF = ((0, 0, 1, 1, 3, 2, 2, 3), (0, 1, 2, 3, 3, 2, 1, 0))


def centre_weight(parity, plane, source):
    residue = BASE[parity][plane // 2]
    if residue == 0:
        residue = 8 * (plane % 2)
        return math.cos(2 * math.pi * (residue * source % 16) / 16)
    angle = 2 * math.pi * (residue * source % 16) / 16
    return -math.sin(angle) if plane % 2 else math.cos(angle)


def packed_pairs(parity):
    return sum(pair << 2 * z for z, pair in enumerate(PAIR_OF[parity]))


def halves(value):
    high = value.astype(BF16)
    return high, (value - high.astype(F32)).astype(BF16)


def kernel(
    x_hbm, apod_ref, coef_ref, off_ref, cos_ref, sin_ref, p_ref, q_ref, out_hbm,
    xe, xh, xl, wide_apod, field, mine, other, planes, spectra, dft_h, dft_l, y_h, y_l, result,
    load_sem, halo_send, halo_recv, own_sem, in_send, in_recv, x_send, x_recv, keep_sem, out_send, out_recv, write_sem,
):
    row, col = lax.axis_index("row"), lax.axis_index("col")
    x_hi, z = row // NZ, row % NZ
    cols = lax.axis_size("col")

    def peer(step):
        return (x_hi * NZ + (z + step) % NZ, col)

    partner = ((1 - x_hi) * NZ + z, col)
    barrier = pltpu.get_barrier_semaphore()
    for step in range(1, NZ):
        pl.semaphore_signal(barrier, inc=1, device_id=peer(step), device_id_type=MESH)
    pl.semaphore_signal(barrier, inc=1, device_id=partner, device_id_type=MESH)

    up, down = (row, (col + 1) % cols), (row, (col + cols - 1) % cols)
    for side in (up, down):
        pl.semaphore_signal(barrier, inc=1, device_id=side, device_id_type=MESH)

    load = pltpu.make_async_copy(x_hbm, xe.at[:, pl.ds(LANES, WIDE)], load_sem)
    load.start()

    for g in range(ROWS // LANES):
        line = jnp.broadcast_to(apod_ref[g : g + 1, :], (LANES, LANES))
        wide_apod[g * LANES : (g + 1) * LANES, :] = line.T

    pl.semaphore_wait(barrier, NZ + 2)

    def halo(side):
        return pltpu.make_async_remote_copy(
            src_ref=x_hbm.at[:, pl.ds((WIDE - LANES) * (1 - side), LANES)],
            dst_ref=xe.at[:, pl.ds((LANES + WIDE) * side, LANES)],
            send_sem=halo_send.at[side],
            recv_sem=halo_recv.at[side],
            device_id=(up, down)[side],
            device_id_type=MESH,
        )

    for side in range(2):
        halo(side).start()

    load.wait()

    def split_tile(t):
        at = pl.ds(t * LANES, LANES)
        high, low = halves(xe[:, at] * wide_apod[...])
        xh[:, at] = high
        xl[:, at] = low

    def stencil_block(b):
        at = pl.ds(pl.multiple_of(b * LANES, LANES), LANES)
        window = pl.ds(pl.multiple_of(b * LANES, LANES), 3 * LANES)
        shape = (3 * LANES, LANES)
        first = lax.broadcasted_iota(jnp.int32, (1, LANES), 1) + LANES + off_ref[:, at]
        tap = lax.broadcasted_iota(jnp.int32, shape, 0) - first
        band = jnp.zeros(shape, F32)
        for q in range(TAPS):
            band = jnp.where(tap == q, coef_ref[q : q + 1, at], band)
        band_h, band_l = halves(band)
        xw = xh[:, window]
        field[b] = (
            jnp.dot(xw, band_h, preferred_element_type=F32)
            + jnp.dot(xw, band_l, preferred_element_type=F32)
            + jnp.dot(xl[:, window], band_h, preferred_element_type=F32)
        )

    def send_in(b):
        pltpu.make_async_copy(
            field.at[b, pl.ds(z * SLAB, SLAB)], mine.at[b, z], own_sem.at[b]
        ).start()
        for step in (4, 3, 5, 2, 6, 1, 7):
            centre = (z + step) % NZ
            pltpu.make_async_remote_copy(
                src_ref=field.at[b, pl.ds(centre * SLAB, SLAB)],
                dst_ref=mine.at[b, z],
                send_sem=in_send.at[b],
                recv_sem=in_recv.at[b],
                device_id=peer(step),
                device_id_type=MESH,
            ).start()

    for t in range(1, NB + 1):
        split_tile(t)

    @pl.loop(2, NB - 1)
    def _(b):
        stencil_block(b)
        send_in(b)

    for side in range(2):
        halo(side).wait_recv()

    @pl.when(col == 0)
    def _():
        xe[:, :LANES] = jnp.zeros((ROWS, LANES), F32)

    @pl.when(col == cols - 1)
    def _():
        xe[:, LANES + WIDE :] = jnp.zeros((ROWS, LANES), F32)

    split_tile(0)
    split_tile(NB + 1)

    @pl.loop(NB - 1, NB + 2)
    def _(i):
        b = i % NB
        stencil_block(b)
        send_in(b)

    @pl.loop(0, 32)
    def _(k):
        c, s = cos_ref[pl.ds(k, 1), :], sin_ref[pl.ds(k, 1), :]
        p, q = p_ref[...], q_ref[...]
        top = halves(c * p - s * q)
        low = halves(-(s * p + c * q))
        for at, (high, rest) in ((0, top), (ROWS, low)):
            rows = pl.ds(pl.multiple_of(at + k * 16, 16), 16)
            dft_h[rows, :] = high
            dft_l[rows, :] = rest

    def exchange(b):
        return pltpu.make_async_remote_copy(
            src_ref=mine.at[b],
            dst_ref=other.at[b],
            send_sem=x_send.at[b],
            recv_sem=x_recv.at[b],
            device_id=partner,
            device_id_type=MESH,
        )

    def pass_on(b):
        pltpu.make_async_copy(field.at[b, pl.ds(0, SLAB)], mine.at[b, z], own_sem.at[b]).wait()
        pltpu.make_async_copy(
            mine.at[b, pl.ds(0, NZ - 1)], mine.at[b, pl.ds(0, NZ - 1)], in_recv.at[b]
        ).wait()
        exchange(b).start()

    sign = (1 - 2 * x_hi).astype(F32)
    weights = [
        [
            jnp.where(x_hi == 0, centre_weight(0, o, s), centre_weight(1, o, s)).astype(F32)
            for s in range(NZ)
        ]
        for o in range(NZ)
    ]
    pairs = packed_pairs(0) + x_hi * (packed_pairs(1) - packed_pairs(0))

    def pair_of(place):
        return lax.shift_right_logical(pairs, 2 * place) & 3

    def centre_of(b):
        exchange(b).wait_recv()
        step = 16
        for part in range(SLAB // step):
            at = pl.ds(part * step, step)
            terms = [other[b, s, at] + sign * mine[b, s, at] for s in range(NZ)]
            for o in range(NZ):
                total = weights[o][0] * terms[0]
                for s in range(1, NZ):
                    total = total + weights[o][s] * terms[s]
                planes[b, o // 2, pl.ds(SLAB * (o % 2) + part * step, step)] = total

    def slot(b):
        return spectra.at[
            b // 2,
            pl.ds(pl.multiple_of(z * LANES, LANES), LANES),
            pl.ds(pl.multiple_of(b % 2 * LANES, LANES), LANES),
        ]

    def send_out(b):
        pltpu.make_async_copy(planes.at[b, pair_of(z)], slot(b), keep_sem.at[b]).start()
        for step in (4, 3, 5, 2, 6, 1, 7):
            pltpu.make_async_remote_copy(
                src_ref=planes.at[b, pair_of((z + step) % NZ)],
                dst_ref=slot(b),
                send_sem=out_send.at[b],
                recv_sem=out_recv.at[b],
                device_id=peer(step),
                device_id_type=MESH,
            ).start()

    pass_on(2)

    @pl.loop(3, NB + 2)
    def _(i):
        pass_on(i % NB)
        b = (i - 1) % NB
        centre_of(b)
        send_out(b)

    centre_of(1)
    send_out(1)

    def write(c):
        return pltpu.make_async_copy(
            result.at[c], out_hbm.at[:, :, pl.ds(pl.multiple_of(c * 256, 256), 256)], write_sem.at[c]
        )

    @pl.loop(1, 5)
    def _(i):
        c = i % 4
        for b in (2 * c, 2 * c + 1):
            pltpu.make_async_copy(planes.at[b, 0], slot(b), keep_sem.at[b]).wait()
            pltpu.make_async_copy(
                spectra.at[c, pl.ds(0, 7 * LANES), pl.ds(0, LANES)],
                spectra.at[c, pl.ds(0, 7 * LANES), pl.ds(0, LANES)],
                out_recv.at[b],
            ).wait()
        high, low = halves(spectra[c])
        y_h[...] = high
        y_l[...] = low
        for part in range(4):
            rows = pl.ds(part * 256, 256)
            result[c, part // 2, pl.ds(part % 2 * 256, 256)] = (
                jnp.dot(dft_h[rows, :], y_h[...], preferred_element_type=F32)
                + jnp.dot(dft_h[rows, :], y_l[...], preferred_element_type=F32)
                + jnp.dot(dft_l[rows, :], y_h[...], preferred_element_type=F32)
            )
        write(c).start()

    for side in range(2):
        halo(side).wait_send()

    @pl.loop(0, NB)
    def _(b):
        seven = mine.at[b, pl.ds(0, NZ - 1)]
        pltpu.make_async_copy(seven, seven, in_send.at[b]).wait()
        exchange(b).wait_send()
        sent = spectra.at[b // 2, pl.ds(0, 7 * LANES), pl.ds(0, LANES)]
        pltpu.make_async_copy(sent, sent, out_send.at[b]).wait()

    for c in range(4):
        write(c).wait()


def tables(x_hi, z):
    lane = jnp.arange(WIDE, dtype=jnp.int32)
    time = SLAB * (lane // LANES) + lane % SLAB
    plane = lane % LANES // SLAB
    residue = 8 * (z % 2) + 4 * (z // 2 % 2) + 2 * (z // 4) + x_hi
    step = jnp.arange(32, dtype=jnp.int32)[:, None]
    turn = 2.0 * math.pi / T1
    coarse = turn * (256 * step * time[None, :] % T1).astype(F32)
    alone = residue % 8 == 0
    quarter = jnp.where((plane == 1) & ~alone, 3 * T1 // 4, 0)
    base = jnp.where(x_hi == 0, residue < 8, residue % 4 == 1)
    size = jnp.where(
        alone,
        jnp.where(plane == residue // 8, 1.0, 0.0),
        jnp.where((plane == 1) & ~base, -1.0, 1.0),
    ) / math.sqrt(T1)
    fine = turn * ((time[None, :] * (16 * step[:16] + residue) + quarter[None, :]) % T1).astype(F32)
    return jnp.cos(coarse), jnp.sin(coarse), size * jnp.cos(fine), size * jnp.sin(fine)


def on_device(signal, apod, coef, block_offset, fine_start):
    row = lax.axis_index("row")
    off = (jnp.repeat(block_offset, WIDE // block_offset.shape[0]) + fine_start)[None, :]
    cosine, sine, p, q = tables(row // NZ, row % NZ)
    vmem, anywhere = (pl.BlockSpec(memory_space=pltpu.VMEM), pl.BlockSpec(memory_space=pl.ANY))
    sem = pltpu.SemaphoreType.DMA
    return pl.pallas_call(
        kernel,
        name="f1_section",
        out_shape=jax.ShapeDtypeStruct((2, ROWS, WIDE), F32),
        in_specs=[anywhere] + [vmem] * 7,
        out_specs=anywhere,
        scratch_shapes=[
            pltpu.VMEM((ROWS, WIDE + 2 * LANES), F32),
            pltpu.VMEM((ROWS, WIDE + 2 * LANES), BF16),
            pltpu.VMEM((ROWS, WIDE + 2 * LANES), BF16),
            pltpu.VMEM((ROWS, LANES), F32),
            pltpu.VMEM((NB, ROWS, LANES), F32),
            pltpu.VMEM((NB, NZ, SLAB, LANES), F32),
            pltpu.VMEM((NB, NZ, SLAB, LANES), F32),
            pltpu.VMEM((NB, 4, LANES, LANES), F32),
            pltpu.VMEM((NB // 2, WIDE, 2 * LANES), F32),
            pltpu.VMEM((WIDE, WIDE), BF16),
            pltpu.VMEM((WIDE, WIDE), BF16),
            pltpu.VMEM((WIDE, 2 * LANES), BF16),
            pltpu.VMEM((WIDE, 2 * LANES), BF16),
            pltpu.VMEM((NB // 2, 2, ROWS, 2 * LANES), F32),
            sem,
            sem((2,)),
            sem((2,)),
            sem((NB,)),
            sem((NB,)),
            sem((NB,)),
            sem((NB,)),
            sem((NB,)),
            sem((NB,)),
            sem((NB,)),
            sem((NB,)),
            sem((4,)),
        ],
        compiler_params=pltpu.CompilerParams(
            collective_id=0, has_side_effects=True, vmem_limit_bytes=56 << 20
        ),
    )(signal, apod.reshape(ROWS // LANES, LANES), coef, off, cosine, sine, p, q)


def solution(mesh):
    placed = (P("row", "col"), P("row"), P(None, "col"), P("col"), P("col"))
    return jax.shard_map(
        on_device, mesh=mesh, in_specs=placed, out_specs=P(None, "row", "col"), check_vma=False
    )
```

time: 271 us -> 160 us (0.59)
  Pallas kernels: 0 us -> 150 us
  waiting for transfers between devices: 100 us -> 0 us
  blocking collectives: 56 us -> 0 us
  matrix products: 39.9 us -> 0 us
  local copies, waits for them, and re-layouts: 35.9 us -> 5.59 us
  starting transfers between devices: 24.6 us -> 0 us
  other arithmetic: 10.9 us -> 3.59 us
    pallas_call x0 -> x1, Pallas kernels: none -> 150 us  [on_device(): pl.pallas_call(kernel, name='f1_section', out_shape=jax.ShapeDtypeStruct(...]
    all_to_all x2 -> x0, waiting for transfers between devices: 98.9 us -> none  [the longest x1 50.2 us: on_device(): lax.all_to_all(field, 'row', split_axis=1, concat_axis=0, tiled=True)]
    all_to_all x1 -> x0, blocking collectives: 56 us -> none  [several_exchanges(): lax.all_to_all(share, axis, split_axis=0, concat_axis=0, tiled=True)]
    dot_general x6 -> x0, matrix products: 39.9 us -> none  [the longest x1 8.6 us: on_device(): jnp.einsum('km,imc->ikc', cosine, rotated_re, precision=HIGH, preferred_e...]
    gather x4 -> x0, local copies, waits for them, and re-layouts: 19.6 us -> none  [apply_stencil(): total = total + coef[tap] * jnp.take(padded, first + tap, axis=-1)]
    all_to_all x2 -> x0, starting transfers between devices: 18.2 us -> none  [the longest x1 11.2 us: on_device(): lax.all_to_all(field, 'row', split_axis=1, concat_axis=0, tiled=True)]
    ppermute x2 -> x0, starting transfers between devices: 6.45 us -> none  [the longest x1 4.54 us: padded_2(): after = lax.ppermute(first, axis, down)]
    reshape x2 -> x1, local copies, waits for them, and re-layouts: 5.42 us -> 0.07 us  [on_device(): jnp.repeat(block_offset, WIDE // block_offset.shape[0]) + fine_start]
  transfers between devices with their start and end apart: 4 -> 0, of which waited for: 3 -> 0; matrix products, arithmetic and copies ran while one was open for 1% -> 0% of each run, Pallas kernels for 0% -> 0%
where the time goes in v1:
time: 160 us; the launch traced here: 159 us
  Pallas kernels  150 us (94%)
  local copies, waits for them, and re-layouts  5.59 us (3%)
  other arithmetic  3.59 us (2%)
    pallas_call x1, Pallas kernels, on_device(): pl.pallas_call(kernel, name='f1_section', out_shape=jax.ShapeDtypeStruct(...  150 us
    unnamed x1, local copies, waits for them, and re-layouts  4.79 us

profile of v1, /device:TPU:8, one launch (start us, length us, event | category | flops | bytes accessed | tf_op | source)
XLA Modules:
  0.0 158.9 jit_solution(16903444234122728031)
XLA Ops:
  0.1 0.7 broadcast_in_dim.30
  0.8 0.1 reshape.69
  0.9 1.3 add.113
  2.1 1.0 sine_multiply_fusion
  3.1 1.3 fusion.6
  4.4 149.7 %f1_section.1 = f32[2,512,1024]{2,1,0:T(8,128)} custom-call(f32[512,1024]{1,0:T(8,128)} %x_hbm.1, f32[4,128]{1,0:T(4,128)} %bitcast.5, f32[4,1024]{1,0:T(4,128)} %coef_ref.1, s32[1,1024]{1,0:T(1,128)} %bitcast.4, f32[32,1024]{1,0:T(8,128)} %get-tuple-element.8.cos_ref, f32[32,1024]{1,0:T(8,128)} %get-tuple-element.7.sin_ref, ...), custom_call_target="tpu_custom_call" | custom-call | tf_op jit(solution)/shard_map/f1_section/pallas_call | solution.py:308
  154.1 4.8 %copy.7 = f32[2,512,1024]{2,1,0:T(8,128)} copy(f32[2,512,1024]{2,1,0:T(8,128)} %f1_section.1) | data formatting | bytes 8388608
  (5 shorter events, 0.0 us)

commit v2 on v1

v2 whole, which is shorter than its diff:
```python
import functools
import math

import jax
import jax.numpy as jnp
import numpy as np
from jax import lax
from jax.experimental import pallas as pl
from jax.experimental.pallas import tpu as pltpu
from jax.sharding import PartitionSpec as P

MESH = pl.DeviceIdType.MESH
TAPS = 4
NZ = 8
NB = 8
LANES = 128
ROWS = 512
SLAB = ROWS // NZ
WIDE = NB * LANES
T1 = 8192
F32, BF16 = jnp.float32, jnp.bfloat16


def residue_of(row):
    digits = row % 2 * 8 + row // 2 % 2 * 4 + row // 4 % 2 * 2 + row // 8
    return digits


NEAR = (-2, -1, 0, 1)
HOPS = 5
START = (None, 0, 5, 9, 12, 14)
TRAVELLING = 15
KEPT = tuple((slab, 0) for slab in NEAR)
SENT = ((-2, 2), (1, -2), (-2, 1), (1, -1))


def sources(slab):
    return [0] + [-hop for hop in range(1, 4 - slab)] + [hop for hop in range(1, 5 + slab)]


def centre_weights():
    table = np.zeros((16, NZ, 2, NZ))
    for row in range(16):
        x_hi, z = divmod(row, NZ)
        for i, (slab, owner) in enumerate(KEPT + SENT):
            residue = residue_of(x_hi * NZ + (z + owner) % NZ)
            for j, source in enumerate(sources(slab)):
                turn = residue * ((z + source) % NZ) % 16
                table[row, i, 0, j] = np.cos(turn * np.pi / 8)
                table[row, i, 1, j] = -np.sin(turn * np.pi / 8) if turn % 8 else 0.0
    return table.reshape(-1).astype(np.float32)


def transform_tables():
    lane = np.arange(WIDE)
    time = SLAB * (lane // LANES) + lane % SLAB
    plane = lane % LANES // SLAB
    coarse = 256 * np.arange(32)[:, None] * time
    fine = 16 * np.arange(16)[:, None] * time
    own = np.array([residue_of(row) for row in range(16)])[:, None] * time - T1 // 4 * plane
    parts = []
    for steps, size in ((coarse, 1.0), (fine, 1.0), (own, 1.0 / math.sqrt(T1))):
        angle = 2.0 * np.pi / T1 * (steps % T1)
        parts += [size * np.cos(angle), size * np.sin(angle)]
    return np.concatenate(parts).astype(np.float32)


def halves(value):
    high = value.astype(BF16)
    return high, (value - high.astype(F32)).astype(BF16)


def kernel(
    weight_ref, block_ref, x_hbm, table_hbm, apod_ref, coef_ref, fine_ref, out_hbm,
    xe, xh, xl, wide_apod, field, other, even, risen, sunk, planes, spectra, table, dft_h, dft_l, y_h, y_l, result,
    load_sem, table_sem, halo_send, halo_recv, x_send, x_recv, up_send, up_recv, down_send, down_recv,
    out_send, out_recv, write_sem,
):
    row, col = lax.axis_index("row"), lax.axis_index("col")
    x_hi, z = row // NZ, row % NZ
    cols = lax.axis_size("col")

    def peer(step):
        return (x_hi * NZ + (z + step + NZ) % NZ, col)

    partner = ((1 - x_hi) * NZ + z, col)
    up, down = (row, (col + 1) % cols), (row, (col + cols - 1) % cols)
    barrier = pltpu.get_barrier_semaphore()
    greeted = [peer(step) for step in (1, 2, -1, -2)] + [partner, up, down]
    for device in greeted:
        pl.semaphore_signal(barrier, inc=1, device_id=device, device_id_type=MESH)

    def load(t):
        return pltpu.make_async_copy(
            x_hbm.at[:, pl.ds((t - 1) * LANES, LANES)], xe.at[:, pl.ds(t * LANES, LANES)], load_sem.at[t]
        )

    for t in (2, 3, 4, 5, 6, 7, 8, 1):
        load(t).start()
    tables = pltpu.make_async_copy(table_hbm, table, table_sem)
    tables.start()

    for g in range(ROWS // LANES):
        line = jnp.broadcast_to(apod_ref[g : g + 1, :], (LANES, LANES))
        wide_apod[g * LANES : (g + 1) * LANES, :] = line.T

    def split_tile(t):
        at = pl.ds(t * LANES, LANES)
        high, low = halves(xe[:, at] * wide_apod[...])
        xh[:, at] = high
        xl[:, at] = low

    def stencil_block(b):
        at, window = pl.ds(b * LANES, LANES), pl.ds(b * LANES, 3 * LANES)
        shape = (3 * LANES, LANES)
        lane = lax.broadcasted_iota(jnp.int32, (1, LANES), 1)
        first = lane + LANES + fine_ref[b : b + 1, :]
        for part in range(4):
            inside = lane // 32 == part
            first = first + jnp.where(inside, block_ref[4 * b + part], 0)
        tap = lax.broadcasted_iota(jnp.int32, shape, 0) - first
        band = jnp.zeros(shape, F32)
        for q in range(TAPS):
            band = jnp.where(tap == q, coef_ref[q : q + 1, at], band)
        band_h, band_l = halves(band)
        xw = xh[:, window]
        field[b] = (
            jnp.dot(xw, band_h, preferred_element_type=F32)
            + jnp.dot(xw, band_l, preferred_element_type=F32)
            + jnp.dot(xl[:, window], band_h, preferred_element_type=F32)
        )

    def exchange(b):
        return pltpu.make_async_remote_copy(
            src_ref=field.at[b],
            dst_ref=other.at[b],
            send_sem=x_send.at[b],
            recv_sem=x_recv.at[b],
            device_id=partner,
            device_id_type=MESH,
        )

    def halo(side):
        return pltpu.make_async_remote_copy(
            src_ref=x_hbm.at[:, pl.ds((WIDE - LANES) * (1 - side), LANES)],
            dst_ref=xe.at[:, pl.ds((LANES + WIDE) * side, LANES)],
            send_sem=halo_send.at[side],
            recv_sem=halo_recv.at[side],
            device_id=(up, down)[side],
            device_id_type=MESH,
        )

    for t in (2, 3):
        load(t).wait()
        split_tile(t)
    for b in range(2, 7):
        load(b + 2).wait()
        split_tile(b + 2)
        stencil_block(b)
        if b == 2:
            pl.semaphore_wait(barrier, len(greeted))
            for side in range(2):
                halo(side).start()
        exchange(b).start()
    load(1).wait()
    split_tile(1)
    stencil_block(1)
    exchange(1).start()

    for side in range(2):
        halo(side).wait_recv()

    @pl.when(col == 0)
    def _():
        xe[:, :LANES] = jnp.zeros((ROWS, LANES), F32)

    @pl.when(col == cols - 1)
    def _():
        xe[:, LANES + WIDE :] = jnp.zeros((ROWS, LANES), F32)

    split_tile(NB + 1)
    stencil_block(7)
    exchange(7).start()
    split_tile(0)
    stencil_block(0)
    exchange(0).start()

    tables.wait()
    own_c, own_s = table[pl.ds(96 + row, 1), :], table[pl.ds(112 + row, 1), :]
    p = table[64:80, :] * own_c - table[80:96, :] * own_s
    q = table[80:96, :] * own_c + table[64:80, :] * own_s
    table[64:80, :] = p
    table[80:96, :] = q

    @pl.loop(0, 32)
    def _(k):
        c, s = table[pl.ds(k, 1), :], table[pl.ds(32 + k, 1), :]
        p, q = table[64:80, :], table[80:96, :]
        top = halves(c * p - s * q)
        low = halves(-(s * p + c * q))
        for at, (high, rest) in ((0, top), (ROWS, low)):
            rows = pl.ds(pl.multiple_of(at + k * 16, 16), 16)
            for i in range(NZ):
                lanes = pl.ds(pl.multiple_of((i - z + 2 + NZ) % NZ * LANES, LANES), LANES)
                dft_h[rows, lanes] = high[:, i * LANES : (i + 1) * LANES]
                dft_l[rows, lanes] = rest[:, i * LANES : (i + 1) * LANES]

    def arrived(ref, sem):
        pltpu.make_async_copy(ref, ref, sem).wait()

    def rise(b, hop):
        if hop == 1:
            source = even.at[b, pl.ds(3, 5)]
        else:
            source = risen.at[b, pl.ds(START[hop - 1] + 1, 6 - hop)]
        return pltpu.make_async_remote_copy(
            src_ref=source,
            dst_ref=risen.at[b, pl.ds(START[hop], 6 - hop)],
            send_sem=up_send.at[b, hop - 1],
            recv_sem=up_recv.at[b, hop - 1],
            device_id=peer(1),
            device_id_type=MESH,
        )

    def sink(b, hop):
        if hop == 1:
            source = even.at[b, pl.ds(0, 5)]
        else:
            source = sunk.at[b, pl.ds(START[hop - 1], 6 - hop)]
        return pltpu.make_async_remote_copy(
            src_ref=source,
            dst_ref=sunk.at[b, pl.ds(START[hop], 6 - hop)],
            send_sem=down_send.at[b, hop - 1],
            recv_sem=down_recv.at[b, hop - 1],
            device_id=peer(-1),
            device_id_type=MESH,
        )

    sign = (1 - 2 * x_hi).astype(F32)

    def depart(b):
        exchange(b).wait_recv()
        for i in range(NZ):
            rows = pl.ds(pl.multiple_of((z + i + 4) % NZ * SLAB, SLAB), SLAB)
            even[b, i] = other[b, rows] + sign * field[b, rows]
        rise(b, 1).start()
        sink(b, 1).start()

    def relay(b, hop):
        rise(b, hop - 1).wait_recv()
        rise(b, hop).start()
        sink(b, hop - 1).wait_recv()
        sink(b, hop).start()

    def terms_of(b, slab, rows):
        terms = [even[b, slab + 4, rows]]
        terms += [risen[b, START[hop] + slab + 2, rows] for hop in range(1, 4 - slab)]
        terms += [sunk[b, START[hop] + slab + 4 - hop, rows] for hop in range(1, 5 + slab)]
        return terms

    def centre_of(b):
        rise(b, HOPS).wait_recv()
        sink(b, HOPS).wait_recv()
        step = 16
        lanes = pl.ds(pl.multiple_of(b % 2 * LANES, LANES), LANES)

        @pl.loop(0, SLAB // step)
        def _(part):
            at = pl.multiple_of(part * step, step)
            for slab in NEAR:
                terms = terms_of(b, slab, pl.ds(at, step))
                for i, (which, owner) in enumerate(KEPT + SENT):
                    if which != slab:
                        continue
                    for plane in range(2):
                        base = ((row * NZ + i) * 2 + plane) * NZ
                        total = weight_ref[base] * terms[0]
                        for j in range(1, NZ):
                            total = total + weight_ref[base + j] * terms[j]
                        if owner == 0:
                            rows = pl.ds((slab + 2) * LANES + SLAB * plane + at, step)
                            spectra[b // 2, rows, lanes] = total
                        else:
                            planes[b, i - len(KEPT), pl.ds(SLAB * plane + at, step)] = total

    def send_out(b):
        for i, (slab, owner) in enumerate(SENT):
            pltpu.make_async_remote_copy(
                src_ref=planes.at[b, i],
                dst_ref=spectra.at[
                    b // 2,
                    pl.ds((slab - owner + 2) % NZ * LANES, LANES),
                    pl.ds(pl.multiple_of(b % 2 * LANES, LANES), LANES),
                ],
                send_sem=out_send.at[b],
                recv_sem=out_recv.at[b],
                device_id=peer(owner),
                device_id_type=MESH,
            ).start()

    def nth(i):
        return jnp.where(i < 5, i + 2, jnp.where(i == 5, 1, 7 * (7 - i)))

    def write(c):
        return pltpu.make_async_copy(
            result.at[c], out_hbm.at[:, :, pl.ds(pl.multiple_of(c * 256, 256), 256)], write_sem.at[c]
        )

    def product(c, near):
        half = pl.ds(0 if near else WIDE // 2, WIDE // 2)
        high, low = halves(spectra[c, half, :])
        y_h[half, :] = high
        y_l[half, :] = low
        for part in range(4):
            rows = pl.ds(part * 256, 256)
            total = (
                jnp.dot(dft_h[rows, half], y_h[half, :], preferred_element_type=F32)
                + jnp.dot(dft_h[rows, half], y_l[half, :], preferred_element_type=F32)
                + jnp.dot(dft_l[rows, half], y_h[half, :], preferred_element_type=F32)
            )
            to = (c, part // 2, pl.ds(part % 2 * 256, 256))
            result[to] = total if near else result[to] + total

    def chunk(i):
        c = jnp.where(i < 2, i + 1, 3 * (3 - i))
        product(c, True)
        for b in (2 * c, 2 * c + 1):
            arrived(planes.at[b], out_recv.at[b])
        product(c, False)
        write(c).start()

    @pl.loop(0, NB + HOPS + 1)
    def _(i):
        for hop in range(HOPS, 1, -1):
            at = i - hop + 1

            @pl.when((at >= 0) & (at < NB))
            def _(at=at, hop=hop):
                relay(nth(at), hop)

        @pl.when(i < NB)
        def _():
            depart(nth(i))

        at = i - HOPS

        @pl.when((at >= 0) & (at < NB))
        def _():
            b = nth(at)
            centre_of(b)
            send_out(b)

        late = i - HOPS - 2

        @pl.when((late > 0) & (late % 2 == 1))
        def _():
            chunk(late // 2)

    chunk(3)

    for side in range(2):
        halo(side).wait_send()

    @pl.loop(0, NB)
    def _(b):
        exchange(b).wait_send()
        for hop in range(1, HOPS + 1):
            rise(b, hop).wait_send()
            sink(b, hop).wait_send()
        arrived(planes.at[b], out_send.at[b])

    for c in range(4):
        write(c).wait()


def on_device(signal, apod, coef, block_offset, fine_start):
    vmem, smem = (pl.BlockSpec(memory_space=pltpu.VMEM), pl.BlockSpec(memory_space=pltpu.SMEM))
    anywhere = pl.BlockSpec(memory_space=pl.ANY)
    sem = pltpu.SemaphoreType.DMA
    extended = WIDE + 2 * LANES
    return pl.pallas_call(
        kernel,
        name="f1_section",
        out_shape=jax.ShapeDtypeStruct((2, ROWS, WIDE), F32),
        in_specs=[smem, smem, anywhere, anywhere, vmem, vmem, vmem],
        out_specs=anywhere,
        scratch_shapes=[
            pltpu.VMEM((ROWS, extended), F32),
            pltpu.VMEM((ROWS, extended), BF16),
            pltpu.VMEM((ROWS, extended), BF16),
            pltpu.VMEM((ROWS, LANES), F32),
            pltpu.VMEM((NB, ROWS, LANES), F32),
            pltpu.VMEM((NB, ROWS, LANES), F32),
            pltpu.VMEM((NB, NZ, SLAB, LANES), F32),
            pltpu.VMEM((NB, TRAVELLING, SLAB, LANES), F32),
            pltpu.VMEM((NB, TRAVELLING, SLAB, LANES), F32),
            pltpu.VMEM((NB, len(SENT), LANES, LANES), F32),
            pltpu.VMEM((NB // 2, WIDE, 2 * LANES), F32),
            pltpu.VMEM((LANES, WIDE), F32),
            pltpu.VMEM((WIDE, WIDE), BF16),
            pltpu.VMEM((WIDE, WIDE), BF16),
            pltpu.VMEM((WIDE, 2 * LANES), BF16),
            pltpu.VMEM((WIDE, 2 * LANES), BF16),
            pltpu.VMEM((NB // 2, 2, ROWS, 2 * LANES), F32),
            sem((NB + 1,)),
            sem,
            sem((2,)),
            sem((2,)),
            sem((NB,)),
            sem((NB,)),
            sem((NB, HOPS)),
            sem((NB, HOPS)),
            sem((NB, HOPS)),
            sem((NB, HOPS)),
            sem((NB,)),
            sem((NB,)),
            sem((4,)),
        ],
        compiler_params=pltpu.CompilerParams(
            collective_id=0, has_side_effects=True, vmem_limit_bytes=60 << 20
        ),
    )(
        centre_weights(),
        block_offset,
        signal,
        transform_tables(),
        apod.reshape(ROWS // LANES, LANES),
        coef,
        fine_start.reshape(NB, LANES),
    )


def solution(mesh):
    placed = (P("row", "col"), P("row"), P(None, "col"), P("col"), P("col"))
    return jax.shard_map(
        on_device, mesh=mesh, in_specs=placed, out_specs=P(None, "row", "col"), check_vma=False
    )
```

time: 160 us -> 153 us (0.956)
  other arithmetic: 3.59 us -> 0 us
  Pallas kernels: 150 us -> 148 us
    pallas_call x1, Pallas kernels: 150 us -> 148 us  [on_device(): pl.pallas_call(kernel, name='f1_section', out_shape=jax.ShapeDtypeStruct(...]
where the time goes in v2:
time: 153 us
  Pallas kernels  148 us (97%)
  local copies, waits for them, and re-layouts  4.79 us (3%)
    pallas_call x1, Pallas kernels, on_device(): pl.pallas_call(kernel, name='f1_section', out_shape=jax.ShapeDtypeStruct(...  148 us
    unnamed x1, local copies, waits for them, and re-layouts  4.79 us

profile of v2, /device:TPU:8, one launch (start us, length us, event | category | flops | bytes accessed | tf_op | source)
XLA Modules:
  0.0 152.9 jit_solution(10000532730877401065)
XLA Ops:
  0.0 148.1 %f1_section.1 = f32[2,512,1024]{2,1,0:T(8,128)} custom-call(f32[2048]{0:T(1024)} %constant.4.clone.weight_ref, s32[32]{0:T(128)} %block_ref.1, f32[512,1024]{1,0:T(8,128)} %x_hbm.1, f32[128,1024]{1,0:T(8,128)} %constant.5.clone.table_hbm, f32[4,128]{1,0:T(4,128)} %bitcast.3, f32[4,1024]{1,0:T(4,128)} %coef_ref.1, s32[8,128]{1,0:T(8,128)} %bitcast.2), custom_call_target="tpu_custom_call" | custom-call | tf_op jit(solution)/shard_map/f1_section/pallas_call | solution.py:381
  148.1 4.8 %copy.9 = f32[2,512,1024]{2,1,0:T(8,128)} copy(f32[2,512,1024]{2,1,0:T(8,128)} %f1_section.1) | data formatting | bytes 8388608

commit v3 on v2

--- a/solution.py
+++ b/solution.py
@@ -28,6 +28,7 @@
 
 NEAR = (-2, -1, 0, 1)
 HOPS = 5
+RAW = 2
 START = (None, 0, 5, 9, 12, 14)
 TRAVELLING = 15
 KEPT = tuple((slab, 0) for slab in NEAR)
@@ -71,10 +72,11 @@
 
 
 def kernel(
-    weight_ref, block_ref, x_hbm, table_hbm, apod_ref, coef_ref, fine_ref, out_hbm,
-    xe, xh, xl, wide_apod, field, other, even, risen, sunk, planes, spectra, table, dft_h, dft_l, y_h, y_l, result,
-    load_sem, table_sem, halo_send, halo_recv, x_send, x_recv, up_send, up_recv, down_send, down_recv,
-    out_send, out_recv, write_sem,
+    weight_hbm, block_hbm, x_hbm, table_hbm, apod_hbm, coef_hbm, fine_hbm, result,
+    weight_ref, block_ref, apod_ref, coef_ref, fine_ref, xe, xh, xl, wide_apod, field, other, even, risen, sunk,
+    other_even, other_risen, other_sunk, planes, spectra, table, dft_h, dft_l, y_h, y_l,
+    small_sem, load_sem, table_sem, halo_send, halo_recv, x_send, x_recv, late_send, late_recv, up_send, up_recv, down_send, down_recv,
+    out_send, out_recv,
 ):
     row, col = lax.axis_index("row"), lax.axis_index("col")
     x_hi, z = row // NZ, row % NZ
@@ -95,10 +97,27 @@
             x_hbm.at[:, pl.ds((t - 1) * LANES, LANES)], xe.at[:, pl.ds(t * LANES, LANES)], load_sem.at[t]
         )
 
+    small = [
+        pltpu.make_async_copy(source, target, small_sem.at[i])
+        for i, (source, target) in enumerate(
+            (
+                (apod_hbm, apod_ref),
+                (coef_hbm, coef_ref),
+                (fine_hbm, fine_ref),
+                (block_hbm, block_ref),
+                (weight_hbm, weight_ref),
+            )
+        )
+    ]
+    for copy in small:
+        copy.start()
     for t in (2, 3, 4, 5, 6, 7, 8, 1):
         load(t).start()
     tables = pltpu.make_async_copy(table_hbm, table, table_sem)
     tables.start()
+
+    for copy in small:
+        copy.wait()
 
     for g in range(ROWS // LANES):
         line = jnp.broadcast_to(apod_ref[g : g + 1, :], (LANES, LANES))
@@ -140,74 +159,6 @@
             device_id_type=MESH,
         )
 
-    def halo(side):
-        return pltpu.make_async_remote_copy(
-            src_ref=x_hbm.at[:, pl.ds((WIDE - LANES) * (1 - side), LANES)],
-            dst_ref=xe.at[:, pl.ds((LANES + WIDE) * side, LANES)],
-            send_sem=halo_send.at[side],
-            recv_sem=halo_recv.at[side],
-            device_id=(up, down)[side],
-            device_id_type=MESH,
-        )
-
-    for t in (2, 3):
-        load(t).wait()
-        split_tile(t)
-    for b in range(2, 7):
-        load(b + 2).wait()
-        split_tile(b + 2)
-        stencil_block(b)
-        if b == 2:
-            pl.semaphore_wait(barrier, len(greeted))
-            for side in range(2):
-                halo(side).start()
-        exchange(b).start()
-    load(1).wait()
-    split_tile(1)
-    stencil_block(1)
-    exchange(1).start()
-
-    for side in range(2):
-        halo(side).wait_recv()
-
-    @pl.when(col == 0)
-    def _():
-        xe[:, :LANES] = jnp.zeros((ROWS, LANES), F32)
-
-    @pl.when(col == cols - 1)
-    def _():
-        xe[:, LANES + WIDE :] = jnp.zeros((ROWS, LANES), F32)
-
-    split_tile(NB + 1)
-    stencil_block(7)
-    exchange(7).start()
-    split_tile(0)
-    stencil_block(0)
-    exchange(0).start()
-
-    tables.wait()
-    own_c, own_s = table[pl.ds(96 + row, 1), :], table[pl.ds(112 + row, 1), :]
-    p = table[64:80, :] * own_c - table[80:96, :] * own_s
-    q = table[80:96, :] * own_c + table[64:80, :] * own_s
-    table[64:80, :] = p
-    table[80:96, :] = q
-
-    @pl.loop(0, 32)
-    def _(k):
-        c, s = table[pl.ds(k, 1), :], table[pl.ds(32 + k, 1), :]
-        p, q = table[64:80, :], table[80:96, :]
-        top = halves(c * p - s * q)
-        low = halves(-(s * p + c * q))
-        for at, (high, rest) in ((0, top), (ROWS, low)):
-            rows = pl.ds(pl.multiple_of(at + k * 16, 16), 16)
-            for i in range(NZ):
-                lanes = pl.ds(pl.multiple_of((i - z + 2 + NZ) % NZ * LANES, LANES), LANES)
-                dft_h[rows, lanes] = high[:, i * LANES : (i + 1) * LANES]
-                dft_l[rows, lanes] = rest[:, i * LANES : (i + 1) * LANES]
-
-    def arrived(ref, sem):
-        pltpu.make_async_copy(ref, ref, sem).wait()
-
     def rise(b, hop):
         if hop == 1:
             source = even.at[b, pl.ds(3, 5)]
@@ -236,6 +187,87 @@
             device_id_type=MESH,
         )
 
+    def depart_raw(b):
+        for i in range(NZ):
+            rows = pl.ds(pl.multiple_of((z + i + 4) % NZ * SLAB, SLAB), SLAB)
+            even[b, i] = field[b, rows]
+        rise(b, 1).start()
+        sink(b, 1).start()
+
+    def halo(side):
+        return pltpu.make_async_remote_copy(
+            src_ref=x_hbm.at[:, pl.ds((WIDE - LANES) * (1 - side), LANES)],
+            dst_ref=xe.at[:, pl.ds((LANES + WIDE) * side, LANES)],
+            send_sem=halo_send.at[side],
+            recv_sem=halo_recv.at[side],
+            device_id=(up, down)[side],
+            device_id_type=MESH,
+        )
+
+    for t in (2, 3):
+        load(t).wait()
+        split_tile(t)
+    for b in range(2, 7):
+        load(b + 2).wait()
+        split_tile(b + 2)
+        stencil_block(b)
+        if b == 2:
+            pl.semaphore_wait(barrier, len(greeted))
+        if b < 2 + RAW:
+            depart_raw(b)
+        else:
+            exchange(b).start()
+        if b == 3:
+            for side in range(2):
+                halo(side).start()
+    load(1).wait()
+    split_tile(1)
+    stencil_block(1)
+    exchange(1).start()
+
+    def outermost():
+        for side in range(2):
+            halo(side).wait_recv()
+
+        @pl.when(col == 0)
+        def _():
+            xe[:, :LANES] = jnp.zeros((ROWS, LANES), F32)
+
+        @pl.when(col == cols - 1)
+        def _():
+            xe[:, LANES + WIDE :] = jnp.zeros((ROWS, LANES), F32)
+
+        split_tile(NB + 1)
+        stencil_block(7)
+        exchange(7).start()
+        split_tile(0)
+        stencil_block(0)
+        exchange(0).start()
+
+    def build_transform():
+        tables.wait()
+        own_c, own_s = table[pl.ds(96 + row, 1), :], table[pl.ds(112 + row, 1), :]
+        p = table[64:80, :] * own_c - table[80:96, :] * own_s
+        q = table[80:96, :] * own_c + table[64:80, :] * own_s
+        table[64:80, :] = p
+        table[80:96, :] = q
+
+        @pl.loop(0, 32)
+        def _(k):
+            c, s = table[pl.ds(k, 1), :], table[pl.ds(32 + k, 1), :]
+            p, q = table[64:80, :], table[80:96, :]
+            top = halves(c * p - s * q)
+            low = halves(-(s * p + c * q))
+            for at, (high, rest) in ((0, top), (ROWS, low)):
+                rows = pl.ds(pl.multiple_of(at + k * 16, 16), 16)
+                for i in range(NZ):
+                    lanes = pl.ds(pl.multiple_of((i - z + 2 + NZ) % NZ * LANES, LANES), LANES)
+                    dft_h[rows, lanes] = high[:, i * LANES : (i + 1) * LANES]
+                    dft_l[rows, lanes] = rest[:, i * LANES : (i + 1) * LANES]
+
+    def arrived(ref, sem):
+        pltpu.make_async_copy(ref, ref, sem).wait()
+
     sign = (1 - 2 * x_hi).astype(F32)
 
     def depart(b):
@@ -252,6 +284,53 @@
         sink(b, hop - 1).wait_recv()
         sink(b, hop).start()
 
+    def late_exchanges(b):
+        r = b - 2
+        return [
+            pltpu.make_async_remote_copy(
+                src_ref=source,
+                dst_ref=target,
+                send_sem=late_send.at[r, i],
+                recv_sem=late_recv.at[r, i],
+                device_id=partner,
+                device_id_type=MESH,
+            )
+            for i, (source, target) in enumerate(
+                (
+                    (even.at[b, pl.ds(2, 4)], other_even.at[r]),
+                    (risen.at[b], other_risen.at[r]),
+                    (sunk.at[b], other_sunk.at[r]),
+                )
+            )
+        ]
+
+    def exchange_late(b):
+        gathered(b)
+        for copy in late_exchanges(b):
+            copy.start()
+
+    def all_passed_on(b):
+        for hop in range(1, HOPS + 1):
+            rise(b, hop).wait_send()
+            sink(b, hop).wait_send()
+
+    def combine_late(b):
+        r = b - 2
+        all_passed_on(b)
+        for copy in late_exchanges(b):
+            copy.wait()
+        for i in range(4):
+            even[b, i + 2] = other_even[r, i] + sign * even[b, i + 2]
+
+        @pl.loop(0, TRAVELLING)
+        def _(i):
+            risen[b, i] = other_risen[r, i] + sign * risen[b, i]
+            sunk[b, i] = other_sunk[r, i] + sign * sunk[b, i]
+
+    def gathered(b):
+        rise(b, HOPS).wait_recv()
+        sink(b, HOPS).wait_recv()
+
     def terms_of(b, slab, rows):
         terms = [even[b, slab + 4, rows]]
         terms += [risen[b, START[hop] + slab + 2, rows] for hop in range(1, 4 - slab)]
@@ -259,8 +338,6 @@
         return terms
 
     def centre_of(b):
-        rise(b, HOPS).wait_recv()
-        sink(b, HOPS).wait_recv()
         step = 16
         lanes = pl.ds(pl.multiple_of(b % 2 * LANES, LANES), LANES)
 
@@ -301,11 +378,6 @@
     def nth(i):
         return jnp.where(i < 5, i + 2, jnp.where(i == 5, 1, 7 * (7 - i)))
 
-    def write(c):
-        return pltpu.make_async_copy(
-            result.at[c], out_hbm.at[:, :, pl.ds(pl.multiple_of(c * 256, 256), 256)], write_sem.at[c]
-        )
-
     def product(c, near):
         half = pl.ds(0 if near else WIDE // 2, WIDE // 2)
         high, low = halves(spectra[c, half, :])
@@ -321,15 +393,13 @@
             to = (c, part // 2, pl.ds(part % 2 * 256, 256))
             result[to] = total if near else result[to] + total
 
-    def chunk(i):
-        c = jnp.where(i < 2, i + 1, 3 * (3 - i))
+    def chunk(c):
         product(c, True)
         for b in (2 * c, 2 * c + 1):
             arrived(planes.at[b], out_recv.at[b])
         product(c, False)
-        write(c).start()
-
-    @pl.loop(0, NB + HOPS + 1)
+
+    @pl.loop(1, NB + HOPS + 1)
     def _(i):
         for hop in range(HOPS, 1, -1):
             at = i - hop + 1
@@ -338,53 +408,81 @@
             def _(at=at, hop=hop):
                 relay(nth(at), hop)
 
-        @pl.when(i < NB)
+        @pl.when((i >= RAW) & (i < NB))
         def _():
             depart(nth(i))
 
+        pl.when(i == 2)(outermost)
+        pl.when(i == 3)(build_transform)
         at = i - HOPS
 
-        @pl.when((at >= 0) & (at < NB))
+        @pl.when((at >= 0) & (at < RAW))
+        def _():
+            exchange_late(nth(at))
+
+        @pl.when((at >= RAW) & (at < NB))
         def _():
             b = nth(at)
+            gathered(b)
             centre_of(b)
             send_out(b)
 
-        late = i - HOPS - 2
-
-        @pl.when((late > 0) & (late % 2 == 1))
-        def _():
-            chunk(late // 2)
-
-    chunk(3)
+        late = i - 9
+
+        @pl.when((late >= 0) & (late < RAW))
+        def _():
+            b = nth(late)
+            combine_late(b)
+            centre_of(b)
+            send_out(b)
+
+        @pl.when((i == 10) | (i == 12) | (i == 13))
+        def _():
+            chunk(jnp.where(i == 10, 2, jnp.where(i == 12, 1, 3)))
+
+    chunk(0)
 
     for side in range(2):
         halo(side).wait_send()
 
     @pl.loop(0, NB)
     def _(b):
-        exchange(b).wait_send()
-        for hop in range(1, HOPS + 1):
-            rise(b, hop).wait_send()
-            sink(b, hop).wait_send()
+
+        @pl.when((b < 2) | (b >= 2 + RAW))
+        def _():
+            exchange(b).wait_send()
+            all_passed_on(b)
+
         arrived(planes.at[b], out_send.at[b])
 
+
+def write_out(result, out_hbm, sem):
+    def write(c):
+        return pltpu.make_async_copy(result.at[c], out_hbm.at[:, :, pl.ds(c * 256, 256)], sem.at[c])
+
+    for c in range(4):
+        write(c).start()
     for c in range(4):
         write(c).wait()
 
 
 def on_device(signal, apod, coef, block_offset, fine_start):
-    vmem, smem = (pl.BlockSpec(memory_space=pltpu.VMEM), pl.BlockSpec(memory_space=pltpu.SMEM))
-    anywhere = pl.BlockSpec(memory_space=pl.ANY)
+    vmem = pl.BlockSpec(memory_space=pltpu.VMEM)
+    anywhere = pl.BlockSpec(memory_space=pltpu.HBM)
     sem = pltpu.SemaphoreType.DMA
     extended = WIDE + 2 * LANES
-    return pl.pallas_call(
+    result = pl.pallas_call(
         kernel,
         name="f1_section",
-        out_shape=jax.ShapeDtypeStruct((2, ROWS, WIDE), F32),
-        in_specs=[smem, smem, anywhere, anywhere, vmem, vmem, vmem],
-        out_specs=anywhere,
+        out_shape=jax.ShapeDtypeStruct((NB // 2, 2, ROWS, 2 * LANES), F32),
+        in_specs=[anywhere] * 7,
+        out_specs=vmem,
         scratch_shapes=[
+            pltpu.SMEM((16 * NZ * 2 * NZ,), F32),
+            pltpu.SMEM(block_offset.shape, jnp.int32),
+            pltpu.VMEM((ROWS // LANES, LANES), F32),
+            pltpu.VMEM((TAPS, WIDE), F32),
+            pltpu.VMEM((NB, LANES), jnp.int32),
             pltpu.VMEM((ROWS, extended), F32),
             pltpu.VMEM((ROWS, extended), BF16),
             pltpu.VMEM((ROWS, extended), BF16),
@@ -394,6 +492,9 @@
             pltpu.VMEM((NB, NZ, SLAB, LANES), F32),
             pltpu.VMEM((NB, TRAVELLING, SLAB, LANES), F32),
             pltpu.VMEM((NB, TRAVELLING, SLAB, LANES), F32),
+            pltpu.VMEM((RAW, len(NEAR), SLAB, LANES), F32),
+            pltpu.VMEM((RAW, TRAVELLING, SLAB, LANES), F32),
+            pltpu.VMEM((RAW, TRAVELLING, SLAB, LANES), F32),
             pltpu.VMEM((NB, len(SENT), LANES, LANES), F32),
             pltpu.VMEM((NB // 2, WIDE, 2 * LANES), F32),
             pltpu.VMEM((LANES, WIDE), F32),
@@ -401,33 +502,48 @@
             pltpu.VMEM((WIDE, WIDE), BF16),
             pltpu.VMEM((WIDE, 2 * LANES), BF16),
             pltpu.VMEM((WIDE, 2 * LANES), BF16),
-            pltpu.VMEM((NB // 2, 2, ROWS, 2 * LANES), F32),
+            sem((5,)),
             sem((NB + 1,)),
             sem,
             sem((2,)),
             sem((2,)),
             sem((NB,)),
             sem((NB,)),
+            sem((RAW, 3)),
+            sem((RAW, 3)),
             sem((NB, HOPS)),
             sem((NB, HOPS)),
             sem((NB, HOPS)),
             sem((NB, HOPS)),
             sem((NB,)),
             sem((NB,)),
-            sem((4,)),
         ],
         compiler_params=pltpu.CompilerParams(
-            collective_id=0, has_side_effects=True, vmem_limit_bytes=60 << 20
+            collective_id=0, has_side_effects=True, vmem_limit_bytes=44 << 20
         ),
     )(
-        centre_weights(),
-        block_offset,
-        signal,
-        transform_tables(),
-        apod.reshape(ROWS // LANES, LANES),
-        coef,
-        fine_start.reshape(NB, LANES),
+        *(
+            pltpu.with_memory_space_constraint(value, pltpu.HBM)
+            for value in (
+                jnp.asarray(centre_weights()),
+                block_offset,
+                signal,
+                jnp.asarray(transform_tables()),
+                apod.reshape(ROWS // LANES, LANES),
+                coef,
+                fine_start.reshape(NB, LANES),
+            )
+        )
     )
+    return pl.pallas_call(
+        write_out,
+        name="write_out",
+        out_shape=jax.ShapeDtypeStruct((2, ROWS, WIDE), F32),
+        in_specs=[vmem],
+        out_specs=anywhere,
+        scratch_shapes=[sem((NB // 2,))],
+        compiler_params=pltpu.CompilerParams(vmem_limit_bytes=16 << 20),
+    )(result)
 
 
 def solution(mesh):

time: 153 us -> 134 us (0.88)
  Pallas kernels: 148 us -> 134 us
  local copies, waits for them, and re-layouts: 4.79 us -> 0 us
    pallas_call x1, Pallas kernels: 148 us -> 132 us  [on_device(): pl.pallas_call(kernel, name='f1_section', out_shape=jax.ShapeDtypeStruct(...]
    unnamed x1 -> x0, local copies, waits for them, and re-layouts: 4.79 us -> none
    pallas_call x0 -> x1, Pallas kernels: none -> 2.04 us  [on_device(): pl.pallas_call(write_out, name='write_out', out_shape=jax.ShapeDtypeStruc...]
where the time goes in v3:
time: 134 us
  Pallas kernels  134 us (100%)
    pallas_call x1, Pallas kernels, on_device(): pl.pallas_call(kernel, name='f1_section', out_shape=jax.ShapeDtypeStruct(...  132 us

profile of v3, /device:TPU:8, one launch (start us, length us, event | category | flops | bytes accessed | tf_op | source)
XLA Modules:
  0.0 134.0 jit_solution(6702563618526124375)
XLA Ops:
  0.0 131.9 %f1_section.1.result = f32[4,2,512,256]{3,2,1,0:T(8,128)S(1)} custom-call(f32[2048]{0:T(1024)} %constant.4.clone.weight_hbm, s32[32]{0:T(128)} %block_hbm.1, f32[512,1024]{1,0:T(8,128)} %x_hbm.1, f32[128,1024]{1,0:T(8,128)} %constant.5.clone.table_hbm, f32[4,128]{1,0:T(4,128)} %bitcast.3, f32[4,1024]{1,0:T(4,128)} %coef_hbm.1, s32[8,128]{1,0:T(8,128)} %bitcast.2), custom_call_target="tpu_custom_call" | custom-call | tf_op jit(solution)/shard_map/f1_section/pallas_call | solution.py:474
  131.9 2.0 %write_out.1 = f32[2,512,1024]{2,1,0:T(8,128)} custom-call(f32[4,2,512,256]{3,2,1,0:T(8,128)S(1)} %f1_section.1.result), custom_call_target="tpu_custom_call" | custom-call | tf_op jit(solution)/shard_map/write_out/pallas_call | solution.py:538

commit v4 on v3

--- a/solution.py
+++ b/solution.py
@@ -71,10 +71,19 @@
     return high, (value - high.astype(F32)).astype(BF16)
 
 
+def three_products(a_h, a_l, b_h, b_l):
+    return (
+        jnp.dot(a_h, b_h, preferred_element_type=F32)
+        + jnp.dot(a_h, b_l, preferred_element_type=F32)
+        + jnp.dot(a_l, b_h, preferred_element_type=F32)
+    )
+
+
 def kernel(
-    weight_hbm, block_hbm, x_hbm, table_hbm, apod_hbm, coef_hbm, fine_hbm, result,
+    weight_hbm, block_hbm, x_hbm, table_hbm, apod_hbm, coef_hbm, fine_hbm,
+    result, far_h, far_l, last_h, last_l,
     weight_ref, block_ref, apod_ref, coef_ref, fine_ref, xe, xh, xl, wide_apod, field, other, even, risen, sunk,
-    other_even, other_risen, other_sunk, planes, spectra, table, dft_h, dft_l, y_h, y_l,
+    other_even, other_risen, other_sunk, planes, spectra, table, turned, near_h, near_l, y_h, y_l,
     small_sem, load_sem, table_sem, halo_send, halo_recv, x_send, x_recv, late_send, late_recv, up_send, up_recv, down_send, down_recv,
     out_send, out_recv,
 ):
@@ -109,14 +118,16 @@
             )
         )
     ]
+    for t in (2, 3, 4):
+        load(t).start()
     for copy in small:
         copy.start()
-    for t in (2, 3, 4, 5, 6, 7, 8, 1):
+    for t in (5, 6, 7, 8, 1):
         load(t).start()
     tables = pltpu.make_async_copy(table_hbm, table, table_sem)
     tables.start()
 
-    for copy in small:
+    for copy in small[:4]:
         copy.wait()
 
     for g in range(ROWS // LANES):
@@ -143,11 +154,7 @@
             band = jnp.where(tap == q, coef_ref[q : q + 1, at], band)
         band_h, band_l = halves(band)
         xw = xh[:, window]
-        field[b] = (
-            jnp.dot(xw, band_h, preferred_element_type=F32)
-            + jnp.dot(xw, band_l, preferred_element_type=F32)
-            + jnp.dot(xl[:, window], band_h, preferred_element_type=F32)
-        )
+        field[b] = three_products(xw, xl[:, window], band_h, band_l)
 
     def exchange(b):
         return pltpu.make_async_remote_copy(
@@ -225,6 +232,8 @@
     stencil_block(1)
     exchange(1).start()
 
+    small[4].wait()
+
     def outermost():
         for side in range(2):
             halo(side).wait_recv()
@@ -252,18 +261,20 @@
         table[64:80, :] = p
         table[80:96, :] = q
 
+        for j in range(NZ):
+            lanes = pl.ds(pl.multiple_of((z + j - 2 + NZ) % NZ * LANES, LANES), LANES)
+            turned[:, j * LANES : (j + 1) * LANES] = table[:96, lanes]
+
         @pl.loop(0, 32)
         def _(k):
-            c, s = table[pl.ds(k, 1), :], table[pl.ds(32 + k, 1), :]
-            p, q = table[64:80, :], table[80:96, :]
+            c, s = turned[pl.ds(k, 1), :], turned[pl.ds(32 + k, 1), :]
+            p, q = turned[64:80, :], turned[80:96, :]
             top = halves(c * p - s * q)
             low = halves(-(s * p + c * q))
-            for at, (high, rest) in ((0, top), (ROWS, low)):
-                rows = pl.ds(pl.multiple_of(at + k * 16, 16), 16)
-                for i in range(NZ):
-                    lanes = pl.ds(pl.multiple_of((i - z + 2 + NZ) % NZ * LANES, LANES), LANES)
-                    dft_h[rows, lanes] = high[:, i * LANES : (i + 1) * LANES]
-                    dft_l[rows, lanes] = rest[:, i * LANES : (i + 1) * LANES]
+            for first, (high, rest) in ((0, top), (ROWS, low)):
+                rows = pl.ds(pl.multiple_of(first + k * 16, 16), 16)
+                near_h[rows, :], far_h[rows, :] = high[:, : WIDE // 2], high[:, WIDE // 2 :]
+                near_l[rows, :], far_l[rows, :] = rest[:, : WIDE // 2], rest[:, WIDE // 2 :]
 
     def arrived(ref, sem):
         pltpu.make_async_copy(ref, ref, sem).wait()
@@ -380,23 +391,21 @@
 
     def product(c, near):
         half = pl.ds(0 if near else WIDE // 2, WIDE // 2)
-        high, low = halves(spectra[c, half, :])
-        y_h[half, :] = high
-        y_l[half, :] = low
+        y_h[...], y_l[...] = halves(spectra[c, half, :])
         for part in range(4):
             rows = pl.ds(part * 256, 256)
-            total = (
-                jnp.dot(dft_h[rows, half], y_h[half, :], preferred_element_type=F32)
-                + jnp.dot(dft_h[rows, half], y_l[half, :], preferred_element_type=F32)
-                + jnp.dot(dft_l[rows, half], y_h[half, :], preferred_element_type=F32)
-            )
+            at_h, at_l = (near_h[rows, :], near_l[rows, :]) if near else (far_h[rows, :], far_l[rows, :])
+            total = three_products(at_h, at_l, y_h[...], y_l[...])
             to = (c, part // 2, pl.ds(part % 2 * 256, 256))
             result[to] = total if near else result[to] + total
 
+    def owned(c):
+        for b in (2 * c, 2 * c + 1):
+            arrived(planes.at[b], out_recv.at[b])
+
     def chunk(c):
         product(c, True)
-        for b in (2 * c, 2 * c + 1):
-            arrived(planes.at[b], out_recv.at[b])
+        owned(c)
         product(c, False)
 
     @pl.loop(1, NB + HOPS + 1)
@@ -427,7 +436,7 @@
             centre_of(b)
             send_out(b)
 
-        late = i - 9
+        late = i - 8
 
         @pl.when((late >= 0) & (late < RAW))
         def _():
@@ -440,7 +449,9 @@
         def _():
             chunk(jnp.where(i == 10, 2, jnp.where(i == 12, 1, 3)))
 
-    chunk(0)
+    product(0, True)
+    owned(0)
+    last_h[...], last_l[...] = halves(spectra[0, pl.ds(WIDE // 2, WIDE // 2), :])
 
     for side in range(2):
         halo(side).wait_send()
@@ -456,14 +467,25 @@
         arrived(planes.at[b], out_send.at[b])
 
 
-def write_out(result, out_hbm, sem):
+def write_out(result, far_h, far_l, last_h, last_l, out_hbm, last, sem):
     def write(c):
         return pltpu.make_async_copy(result.at[c], out_hbm.at[:, :, pl.ds(c * 256, 256)], sem.at[c])
 
-    for c in range(4):
+    def write_part(part):
+        at = (part // 2, pl.ds(part % 2 * 256, 256))
+        return pltpu.make_async_copy(last.at[at], out_hbm.at[*at, pl.ds(0, 256)], sem.at[4 + part])
+
+    for c in range(1, 4):
         write(c).start()
-    for c in range(4):
+    for part in range(4):
+        at, rows = (part // 2, pl.ds(part % 2 * 256, 256)), pl.ds(part * 256, 256)
+        total = three_products(far_h[rows, :], far_l[rows, :], last_h[...], last_l[...])
+        last[at] = result[0, *at] + total
+        write_part(part).start()
+    for c in range(1, 4):
         write(c).wait()
+    for part in range(4):
+        write_part(part).wait()
 
 
 def on_device(signal, apod, coef, block_offset, fine_start):
@@ -471,12 +493,18 @@
     anywhere = pl.BlockSpec(memory_space=pltpu.HBM)
     sem = pltpu.SemaphoreType.DMA
     extended = WIDE + 2 * LANES
-    result = pl.pallas_call(
+    done = pl.pallas_call(
         kernel,
         name="f1_section",
-        out_shape=jax.ShapeDtypeStruct((NB // 2, 2, ROWS, 2 * LANES), F32),
+        out_shape=[
+            jax.ShapeDtypeStruct((NB // 2, 2, ROWS, 2 * LANES), F32),
+            jax.ShapeDtypeStruct((WIDE, WIDE // 2), BF16),
+            jax.ShapeDtypeStruct((WIDE, WIDE // 2), BF16),
+            jax.ShapeDtypeStruct((WIDE // 2, 2 * LANES), BF16),
+            jax.ShapeDtypeStruct((WIDE // 2, 2 * LANES), BF16),
+        ],
         in_specs=[anywhere] * 7,
-        out_specs=vmem,
+        out_specs=[vmem] * 5,
         scratch_shapes=[
             pltpu.SMEM((16 * NZ * 2 * NZ,), F32),
             pltpu.SMEM(block_offset.shape, jnp.int32),
@@ -498,10 +526,11 @@
             pltpu.VMEM((NB, len(SENT), LANES, LANES), F32),
             pltpu.VMEM((NB // 2, WIDE, 2 * LANES), F32),
             pltpu.VMEM((LANES, WIDE), F32),
-            pltpu.VMEM((WIDE, WIDE), BF16),
-            pltpu.VMEM((WIDE, WIDE), BF16),
-            pltpu.VMEM((WIDE, 2 * LANES), BF16),
-            pltpu.VMEM((WIDE, 2 * LANES), BF16),
+            pltpu.VMEM((96, WIDE), F32),
+            pltpu.VMEM((WIDE, WIDE // 2), BF16),
+            pltpu.VMEM((WIDE, WIDE // 2), BF16),
+            pltpu.VMEM((WIDE // 2, 2 * LANES), BF16),
+            pltpu.VMEM((WIDE // 2, 2 * LANES), BF16),
             sem((5,)),
             sem((NB + 1,)),
             sem,
@@ -539,11 +568,11 @@
         write_out,
         name="write_out",
         out_shape=jax.ShapeDtypeStruct((2, ROWS, WIDE), F32),
-        in_specs=[vmem],
+        in_specs=[vmem] * 5,
         out_specs=anywhere,
-        scratch_shapes=[sem((NB // 2,))],
+        scratch_shapes=[pltpu.VMEM((2, ROWS, 2 * LANES), F32), sem((8,))],
         compiler_params=pltpu.CompilerParams(vmem_limit_bytes=16 << 20),
-    )(result)
+    )(*done)
 
 
 def solution(mesh):

time: 134 us -> 133 us (level)
  no operation moved by 1% of the time
where the time goes in v4:
time: 133 us
  Pallas kernels  133 us (100%)
    pallas_call x1, Pallas kernels, on_device(): pl.pallas_call(kernel, name='f1_section', out_shape=[jax.ShapeDtypeStruct...  131 us

profile of v4, /device:TPU:8, one launch (start us, length us, event | category | flops | bytes accessed | tf_op | source)
XLA Modules:
  0.0 133.2 jit_solution(10780595702044836583)
XLA Ops:
  0.0 131.1 %f1_section.1 = (f32[4,2,512,256]{3,2,1,0:T(8,128)S(1)}, bf16[1024,512]{1,0:T(8,128)(2,1)S(1)}, bf16[1024,512]{1,0:T(8,128)(2,1)S(1)}, bf16[512,256]{1,0:T(8,128)(2,1)S(1)}, bf16[512,256]{1,0:T(8,128)(2,1)S(1)}) custom-call(f32[2048]{0:T(1024)} %constant.4.clone.weight_hbm, s32[32]{0:T(128)} %block_hbm.1, f32[512,1024]{1,0:T(8,128)} %x_hbm.1, ...), custom_call_target="tpu_custom_call" | custom-call | tf_op jit(solution)/shard_map/f1_section/pallas_call | solution.py:496
  131.1 2.1 %write_out.1 = f32[2,512,1024]{2,1,0:T(8,128)} custom-call(f32[4,2,512,256]{3,2,1,0:T(8,128)S(1)} %get-tuple-element.10.result, bf16[1024,512]{1,0:T(8,128)(2,1)S(1)} %get-tuple-element.11.far_h, bf16[1024,512]{1,0:T(8,128)(2,1)S(1)} %get-tuple-element.12.far_l, bf16[512,256]{1,0:T(8,128)(2,1)S(1)} %get-tuple-element.13.last_h, ...), custom_call_target="tpu_custom_call" | custom-call | tf_op jit(solution)/shard_map/write_out/pallas_call | solution.py:567

commit v5 on v4

--- a/solution.py
+++ b/solution.py
@@ -211,12 +211,13 @@
             device_id_type=MESH,
         )
 
-    for t in (2, 3):
-        load(t).wait()
-        split_tile(t)
-    for b in range(2, 7):
-        load(b + 2).wait()
-        split_tile(b + 2)
+    ready = []
+    for b in (2, 4, 3, 5, 6):
+        for t in range(b, b + 3):
+            if t not in ready:
+                load(t).wait()
+                split_tile(t)
+                ready.append(t)
         stencil_block(b)
         if b == 2:
             pl.semaphore_wait(barrier, len(greeted))
@@ -224,9 +225,8 @@
             depart_raw(b)
         else:
             exchange(b).start()
-        if b == 3:
-            for side in range(2):
-                halo(side).start()
+    for side in range(2):
+        halo(side).start()
     load(1).wait()
     split_tile(1)
     stencil_block(1)
@@ -309,8 +309,9 @@
             for i, (source, target) in enumerate(
                 (
                     (even.at[b, pl.ds(2, 4)], other_even.at[r]),
-                    (risen.at[b], other_risen.at[r]),
-                    (sunk.at[b], other_sunk.at[r]),
+                    (risen.at[b, pl.ds(0, 4)], other_risen.at[r, pl.ds(0, 4)]),
+                    (risen.at[b, pl.ds(5, 10)], other_risen.at[r, pl.ds(5, 10)]),
+                    (sunk.at[b, pl.ds(1, 14)], other_sunk.at[r, pl.ds(1, 14)]),
                 )
             )
         ]
@@ -333,10 +334,11 @@
         for i in range(4):
             even[b, i + 2] = other_even[r, i] + sign * even[b, i + 2]
 
-        @pl.loop(0, TRAVELLING)
+        @pl.loop(0, TRAVELLING - 1)
         def _(i):
-            risen[b, i] = other_risen[r, i] + sign * risen[b, i]
-            sunk[b, i] = other_sunk[r, i] + sign * sunk[b, i]
+            up, down = jnp.where(i < 4, i, i + 1), i + 1
+            risen[b, up] = other_risen[r, up] + sign * risen[b, up]
+            sunk[b, down] = other_sunk[r, down] + sign * sunk[b, down]
 
     def gathered(b):
         rise(b, HOPS).wait_recv()
@@ -421,7 +423,7 @@
         def _():
             depart(nth(i))
 
-        pl.when(i == 2)(outermost)
+        pl.when(i == 4)(outermost)
         pl.when(i == 3)(build_transform)
         at = i - HOPS
 
@@ -445,9 +447,9 @@
             centre_of(b)
             send_out(b)
 
-        @pl.when((i == 10) | (i == 12) | (i == 13))
-        def _():
-            chunk(jnp.where(i == 10, 2, jnp.where(i == 12, 1, 3)))
+        @pl.when((i == 10) | (i == 11) | (i == 13))
+        def _():
+            chunk(jnp.where(i == 10, 2, jnp.where(i == 11, 1, 3)))
 
     product(0, True)
     owned(0)
@@ -538,8 +540,8 @@
             sem((2,)),
             sem((NB,)),
             sem((NB,)),
-            sem((RAW, 3)),
-            sem((RAW, 3)),
+            sem((RAW, 4)),
+            sem((RAW, 4)),
             sem((NB, HOPS)),
             sem((NB, HOPS)),
             sem((NB, HOPS)),

time: 133 us -> 133 us (level)
  no operation moved by 1% of the time
where the time goes in v5:
time: 133 us
  Pallas kernels  133 us (100%)
    pallas_call x1, Pallas kernels, on_device(): pl.pallas_call(kernel, name='f1_section', out_shape=[jax.ShapeDtypeStruct...  131 us

profile of v5, /device:TPU:8, one launch (start us, length us, event | category | flops | bytes accessed | tf_op | source)
XLA Modules:
  0.0 133.3 jit_solution(7831953632026425815)
XLA Ops:
  0.0 131.2 %f1_section.1 = (f32[4,2,512,256]{3,2,1,0:T(8,128)S(1)}, bf16[1024,512]{1,0:T(8,128)(2,1)S(1)}, bf16[1024,512]{1,0:T(8,128)(2,1)S(1)}, bf16[512,256]{1,0:T(8,128)(2,1)S(1)}, bf16[512,256]{1,0:T(8,128)(2,1)S(1)}) custom-call(f32[2048]{0:T(1024)} %constant.4.clone.weight_hbm, s32[32]{0:T(128)} %block_hbm.1, f32[512,1024]{1,0:T(8,128)} %x_hbm.1, ...), custom_call_target="tpu_custom_call" | custom-call | tf_op jit(solution)/shard_map/f1_section/pallas_call | solution.py:498
  131.2 2.1 %write_out.1 = f32[2,512,1024]{2,1,0:T(8,128)} custom-call(f32[4,2,512,256]{3,2,1,0:T(8,128)S(1)} %get-tuple-element.10.result, bf16[1024,512]{1,0:T(8,128)(2,1)S(1)} %get-tuple-element.11.far_h, bf16[1024,512]{1,0:T(8,128)(2,1)S(1)} %get-tuple-element.12.far_l, bf16[512,256]{1,0:T(8,128)(2,1)S(1)} %get-tuple-element.13.last_h, ...), custom_call_target="tpu_custom_call" | custom-call | tf_op jit(solution)/shard_map/write_out/pallas_call | solution.py:569
